TPU v7x, 256 devices: a whole 4x4x8 slice. The times are simulated.
256 devices in a mesh: space: 64 (over x, z, core), chan: 4 (over y).
Axes of the slice: x: 4, y: 4, z: 8, core: 2. Of those that a mesh axis runs over, the one named last changes fastest.
Arguments:
- features: bfloat16 [8192, 512], P('space', 'chan'), may hold values from -6 to 6
- mask: int32 [8192], P('space'), may hold values 0 or 1
- rulebook: int32 [128, 27], P('space'), may hold values from -1 to 127, as said below
- weight_first: bfloat16 [512, 27, 512], P('space', None, 'chan'), may hold values from -0.0546875 to 0.0546875
- weight_second: bfloat16 [512, 27, 512], P('space', None, 'chan'), may hold values from -0.0546875 to 0.0546875
- cotangent: bfloat16 [8192, 512], P('space', 'chan'), may hold values from -6 to 6
Outputs:
- output: bfloat16 [8192, 512], P('space', 'chan')
- features_grad: bfloat16 [8192, 512], P('space', 'chan')
- weight_first_grad: float32 [512, 27, 512], P('space', None, 'chan')
- weight_second_grad: float32 [512, 27, 512], P('space', None, 'chan')
Inputs may be any that keep to these rules, and one draw needn't show every extreme that they name: `rulebook`: entry [b, c] is the brick that feeds brick b through brick offset c, or -1 for none; entry 13 is b itself. A brick of another device belongs to a device s one or two indices away; if it feeds the device s + 1, s + 2, s - 1 or s - 2 (k = 0, 1, 2, 3 respectively), it is brick s * 2 + ((k + h) mod 2) for some h below 1.
All inputs are finite; a program needn't handle non-finite values. No bound on the sum of `mask` on one device may be relied on, other than what follows from the above.
Results may differ from a plain program's by a relative error of at most 0.005.
Values may be sent and summed in bfloat16 or wider, within the bound.
No kernel may reach another device: no remote copies, remote signals or barrier semaphores. Data moves between devices by JAX's collectives and lax.ppermute only.
A program may use at most 128 MiB of HBM per device.

v0:
```python
import jax
import jax.numpy as jnp
import numpy as np
from jax import lax
from jax.sharding import PartitionSpec as P

HB = 1
direction_steps = (1, 2, -1, -2)


def passed_along(value, axis, by):
    devices = lax.axis_size(axis)
    pairs = [(i, i + by) for i in range(devices) if 0 <= i + by < devices]
    return lax.ppermute(value, axis, pairs)


def offset_tables():
    brick_table = np.zeros((27, 64), np.int32)
    cell_table = np.zeros((27, 64), np.int32)
    for offset in range(27):
        moves = (offset // 9 - 1, offset // 3 % 3 - 1, offset % 3 - 1)
        for voxel in range(64):
            cells = (voxel // 16, voxel // 4 % 4, voxel % 4)
            target = [cells[axis_number] + moves[axis_number] for axis_number in range(3)]
            brick_table[offset, voxel] = (
                (target[0] // 4 + 1) * 9 + (target[1] // 4 + 1) * 3 + (target[2] // 4 + 1)
            )
            cell_table[offset, voxel] = target[0] % 4 * 16 + target[1] % 4 * 4 + target[2] % 4
    return (brick_table, cell_table)


def on_device(features, mask, rulebook, weight_first, weight_second, cotangent):
    brick_table, cell_table = offset_tables()
    bricks = rulebook.shape[0]
    spread = HB
    row_count = features.shape[0]
    halo_rows = 4 * spread * 64
    device_index = lax.axis_index("space")
    owner_device = rulebook // bricks
    within = rulebook % bricks
    sources = device_index - jnp.array(direction_steps, jnp.int32)
    lent_table = (
        jnp.arange(4, dtype=jnp.int32)[:, None] * spread
        + jnp.arange(spread, dtype=jnp.int32)[None, :]
    ) % bricks
    matches = (owner_device[:, :, None, None] == sources[None, None, :, None]) & (
        within[:, :, None, None] == lent_table[None, None]
    )
    numbers = bricks + jnp.arange(4 * spread, dtype=jnp.int32).reshape(4, spread)
    remote = jnp.sum(jnp.where(matches, numbers, 0), axis=(2, 3))
    slot_index = jnp.where(
        rulebook < 0, bricks + 4 * spread, jnp.where(owner_device == device_index, within, remote)
    )
    lookup = slot_index[:, brick_table] * 64 + cell_table[None]
    lookup = jnp.transpose(lookup, (1, 0, 2)).reshape(27, row_count).astype(jnp.int32)
    active = mask.astype(jnp.float32)[:, None]
    masked = (features.astype(jnp.float32) * active).astype(jnp.bfloat16)

    def outgoing(source, position):
        shaped = source.reshape(bricks, 64, source.shape[1])
        return jnp.take(shaped, lent_table[position], axis=0).reshape(spread * 64, source.shape[1])

    def extend(source):
        gathered = lax.all_gather(source, "chan", axis=1, tiled=True)
        blocks = [gathered]
        for position, offset in enumerate(direction_steps):
            blocks.append(passed_along(outgoing(gathered, position), "space", offset))
        blocks.append(jnp.zeros((64, gathered.shape[1]), jnp.bfloat16))
        return jnp.concatenate(blocks, 0)

    def lend_back(own_rows, returned, position):
        shaped = own_rows.reshape(bricks, 64, own_rows.shape[1])
        shaped = shaped.at[lent_table[position]].add(
            returned.reshape(spread, 64, own_rows.shape[1])
        )
        return shaped.reshape(row_count, own_rows.shape[1])

    def settle(running):
        summed = lax.psum_scatter(
            running[: row_count + halo_rows], "chan", scatter_dimension=1, tiled=True
        )
        own_rows = summed[:row_count]
        for position, offset in enumerate(direction_steps):
            block_start = row_count + position * spread * 64
            returned = passed_along(
                summed[block_start : block_start + spread * 64], "space", -offset
            )
            own_rows = lend_back(own_rows, returned, position)
        return own_rows

    def weight_term(extended, gradient):

        def advance(offset):
            picked = jnp.take(extended, lookup[offset], axis=0)
            return lax.dot_general(
                picked, gradient, (((0,), (0,)), ((), ())), preferred_element_type=jnp.float32
            )

        stacked = lax.map(advance, jnp.arange(27, dtype=jnp.int32))
        return jnp.transpose(stacked, (1, 0, 2))

    ext_in = extend(masked)
    table_rows = ext_in.shape[0]
    width = ext_in.shape[1]
    initial = jnp.zeros((row_count, weight_first.shape[2]), jnp.float32)
    segment = lax.all_gather(weight_first, "space", axis=0, tiled=True)
    columns = ext_in

    def advance(offset, running):
        picked = jnp.take(columns, lookup[offset], axis=0)
        kernel = lax.dynamic_index_in_dim(segment, offset, 1, keepdims=False)
        return running + jnp.dot(picked, kernel, preferred_element_type=jnp.float32)

    first_act = active * lax.fori_loop(0, 27, advance, initial)
    hidden = jax.nn.silu(first_act).astype(jnp.bfloat16)
    ext_hidden = extend(hidden)
    second_whole = lax.all_gather(weight_second, "space", axis=0, tiled=True)

    def forward_step(offset, running):
        picked = jnp.take(ext_hidden, lookup[offset], axis=0)
        kernel = lax.dynamic_index_in_dim(second_whole, offset, 1, keepdims=False)
        return running + jnp.dot(picked, kernel, preferred_element_type=jnp.float32)

    second_act = active * lax.fori_loop(
        0, 27, forward_step, jnp.zeros((row_count, second_whole.shape[2]), jnp.float32)
    )
    output = second_act.astype(jnp.bfloat16)
    grad_second = (cotangent.astype(jnp.float32) * active).astype(jnp.bfloat16)
    weight_second_grad = lax.psum_scatter(
        weight_term(ext_hidden, grad_second), "space", scatter_dimension=0, tiled=True
    )

    def backward_step(offset, running):
        kernel = lax.dynamic_index_in_dim(second_whole, offset, 1, keepdims=False)
        contrib = lax.dot_general(
            grad_second, kernel, (((1,), (1,)), ((), ())), preferred_element_type=jnp.float32
        )
        return running.at[lookup[offset]].add(contrib)

    hidden_grad = settle(
        lax.fori_loop(0, 27, backward_step, jnp.zeros((table_rows, width), jnp.float32))
    )
    sigmoid_first = jax.nn.sigmoid(first_act)
    grad_first = (
        active * hidden_grad * sigmoid_first * (1.0 + first_act * (1.0 - sigmoid_first))
    ).astype(jnp.bfloat16)
    weight_first_grad = lax.psum_scatter(
        weight_term(ext_in, grad_first), "space", scatter_dimension=0, tiled=True
    )

    def add_back(running, segment):
        columns = running

        def advance(offset, current):
            kernel = lax.dynamic_index_in_dim(segment, offset, 1, keepdims=False)
            contrib = lax.dot_general(
                grad_first, kernel, (((1,), (1,)), ((), ())), preferred_element_type=jnp.float32
            )
            return current.at[lookup[offset]].add(contrib)

        columns = lax.fori_loop(0, 27, advance, columns)
        return columns

    running = add_back(
        jnp.zeros((table_rows, width), jnp.float32),
        lax.all_gather(weight_first, "space", axis=0, tiled=True),
    )
    features_grad = (active * settle(running)).astype(jnp.bfloat16)
    return (output, features_grad, weight_first_grad, weight_second_grad)


def solution(mesh):
    placed = (
        P("space", "chan"),
        P("space"),
        P("space", None),
        P("space", None, "chan"),
        P("space", None, "chan"),
        P("space", "chan"),
    )
    return jax.shard_map(
        on_device,
        mesh=mesh,
        in_specs=placed,
        out_specs=(
            P("space", "chan"),
            P("space", "chan"),
            P("space", None, "chan"),
            P("space", None, "chan"),
        ),
        check_vma=False,
    )
```

profile of v0, /device:TPU:8, one launch (start us, length us, event | category | flops | bytes accessed | tf_op | source)
XLA Modules:
  0.0 875.7 jit_solution(18097774328851206864)
XLA Ops:
  10.5 3.3 gather_fusion.4
  16.8 71.8 %all-gather.5.cloned.1.call-done = bf16[512,27,128]{2,0,1:T(8,128)(2,1)} async-done(((bf16[8,27,128]{2,0,1:T(8,128)(2,1)}), bf16[512,27,128]{2,0,1:T(8,128)(2,1)}) %all-gather.5.cloned.1.call-update) | async-done | bytes 3538960 | tf_op jit(solution)/shard_map/all_gather | solution.py:117
  88.7 80.3 %while.83 = (s32[]{:T(128)}, f32[448,512]{1,0:T(8,128)S(1)}, s32[27,128]{1,0:T(8,128)S(1)}, bf16[512,27,128]{2,0,1:T(8,128)(2,1)}, bf16[128,128]{1,0:T(8,128)(2,1)S(1)}, /*index=5*/s32[]{:T(128)}) while((s32[]{:T(128)}, f32[448,512]{1,0:T(8,128)S(1)}, s32[27,128]{1,0:T(8,128)S(1)}, bf16[512,27,128]{2,0,1:T(8,128)(2,1)}, ...), condition=%wide.region_7.10_spmd, body=%wide.region_5.9_spmd.sunk | while | flops 16843136 | bytes 1738325 | solution.py:141
  90.0 1.7 scatter_fusion
  93.0 1.7 scatter_fusion
  96.0 1.7 scatter_fusion
  98.9 1.7 scatter_fusion
  101.9 1.7 scatter_fusion
  104.9 1.7 scatter_fusion
  107.8 1.7 scatter_fusion
  110.8 1.7 scatter_fusion
  113.8 1.7 scatter_fusion
  116.8 1.7 scatter_fusion
  119.7 1.7 scatter_fusion
  122.7 1.7 scatter_fusion
  125.7 1.7 scatter_fusion
  128.7 1.7 scatter_fusion
  131.6 1.7 scatter_fusion
  134.6 1.7 scatter_fusion
  137.6 1.7 scatter_fusion
  140.5 1.7 scatter_fusion
  143.5 1.7 scatter_fusion
  146.5 1.7 scatter_fusion
  149.5 1.7 scatter_fusion
  152.4 1.7 scatter_fusion
  158.4 1.7 scatter_fusion
  161.3 1.7 scatter_fusion
  167.3 1.7 scatter_fusion
  179.1 11.7 %all_gather.13 = bf16[128,512]{1,0:T(8,128)(2,1)S(1)} all-gather(bf16[128,128]{1,0:T(8,128)(2,1)S(1)} %get-tuple-element.700), channel_id=1, replica_groups=mesh['space'=64,'chan'=4] {'chan'}, dimensions={1}, use_global_device_ids=true | all-gather | bytes 163840 | tf_op jit(solution)/shard_map/all_gather | solution.py:64
  192.1 4.1 collective-permute-start.1
  199.8 5.2 collective-permute-done.3
  207.2 65.6 %all-gather.3.cloned.1.call-done = bf16[512,27,128]{2,0,1:T(8,128)(2,1)} async-done(((bf16[8,27,128]{2,0,1:T(8,128)(2,1)}), bf16[512,27,128]{2,0,1:T(8,128)(2,1)}) %all-gather.3.cloned.1.call-update) | async-done | bytes 3538960 | tf_op jit(solution)/shard_map/all_gather | solution.py:106
  272.7 55.7 %while.87 = (s32[]{:T(128)}, f32[128,128]{1,0:T(8,128)S(1)}, s32[27,128]{1,0:T(8,128)S(1)}, bf16[448,512]{1,0:T(8,128)(2,1)S(1)}, bf16[512,27,128]{2,0,1:T(8,128)(2,1)}, /*index=5*/s32[]{:T(128)}, s32[]{:T(128)}) while((s32[]{:T(128)}, f32[128,128]{1,0:T(8,128)S(1)}, s32[27,128]{1,0:T(8,128)S(1)}, bf16[448,512]{1,0:T(8,128)(2,1)S(1)}, ...), condition=%wide.region_2.5_spmd.clone, body=%wide.region_1.4_spmd.clone.sunk | while | flops 16877316 | bytes 661863 | solution.py:114
  329.8 2.2 collective-permute-start.10
  332.0 4.3 collective-permute-start.11
  339.1 80.3 %while.84 = (s32[]{:T(128)}, f32[448,512]{1,0:T(8,128)S(1)}, s32[27,128]{1,0:T(8,128)S(1)}, bf16[512,27,128]{2,0,1:T(8,128)(2,1)}, bf16[128,128]{1,0:T(8,128)(2,1)S(1)}, /*index=5*/s32[]{:T(128)}) while((s32[]{:T(128)}, f32[448,512]{1,0:T(8,128)S(1)}, s32[27,128]{1,0:T(8,128)S(1)}, bf16[512,27,128]{2,0,1:T(8,128)(2,1)}, ...), condition=%wide.region_15.18_spmd, body=%wide.region_13.17_spmd.sunk | while | flops 16843136 | bytes 1738325 | solution.py:161
  343.4 1.7 scatter_fusion.1
  346.3 1.7 scatter_fusion.1
  349.3 1.7 scatter_fusion.1
  352.3 1.7 scatter_fusion.1
  358.2 1.7 scatter_fusion.1
  364.2 1.7 scatter_fusion.1
  367.2 1.7 scatter_fusion.1
  370.1 1.7 scatter_fusion.1
  373.1 1.7 scatter_fusion.1
  379.0 1.7 scatter_fusion.1
  385.0 1.7 scatter_fusion.1
  388.0 1.7 scatter_fusion.1
  393.9 1.7 scatter_fusion.1
  399.9 1.7 scatter_fusion.1
  402.8 1.7 scatter_fusion.1
  405.8 1.7 scatter_fusion.1
  408.8 1.7 scatter_fusion.1
  414.7 1.7 scatter_fusion.1
  420.4 11.2 %all_gather.15 = bf16[128,512]{1,0:T(8,128)(2,1)S(1)} all-gather(bf16[128,128]{1,0:T(8,128)(2,1)S(1)} %get-tuple-element.688), channel_id=1, replica_groups=mesh['space'=64,'chan'=4] {'chan'}, dimensions={1}, use_global_device_ids=true | all-gather | bytes 163840 | tf_op jit(solution)/shard_map/all_gather | solution.py:64
  433.0 4.3 collective-permute-start.5
  439.9 3.7 broadcast.332.clone
  443.6 119.1 %while.85 = (s32[]{:T(128)}, f32[27,512,128]{2,1,0:T(8,128)}, s32[27]{0:T(128)S(1)}, s32[27,128]{1,0:T(8,128)S(1)}, bf16[448,512]{1,0:T(8,128)(2,1)S(1)}, /*inde...) while((s32[]{:T(128)}, f32[27,512,128]{2,1,0:T(8,128)}, s32[27]{0:T(128)S(1)}, ...), condition=%wide.region_18.21_spmd, body=%wide.region_17.20_spmd.sunk | while | flops 16844548 | bytes 694683 | solution.py:99
  563.0 3.7 broadcast.332.clone.1
  566.6 119.1 %while.86 = (s32[]{:T(128)}, f32[27,512,128]{2,1,0:T(8,128)}, s32[27]{0:T(128)S(1)}, s32[27,128]{1,0:T(8,128)S(1)}, bf16[448,512]{1,0:T(8,128)(2,1)S(1)}, /*inde...) while((s32[]{:T(128)}, f32[27,512,128]{2,1,0:T(8,128)}, s32[27]{0:T(128)S(1)}, ...), condition=%wide.region_21.24_spmd, body=%wide.region_20.23_spmd.sunk | while | flops 16844548 | bytes 694683 | solution.py:99
  687.9 55.8 %while.88 = (s32[]{:T(128)}, f32[128,128]{1,0:T(8,128)S(1)}, s32[27,128]{1,0:T(8,128)S(1)}, bf16[448,512]{1,0:T(8,128)(2,1)S(1)}, bf16[512,27,128]{2,0,1:T(8,128)(2,1)}, /*index=5*/s32[]{:T(128)}, s32[]{:T(128)}) while((s32[]{:T(128)}, f32[128,128]{1,0:T(8,128)S(1)}, s32[27,128]{1,0:T(8,128)S(1)}, bf16[448,512]{1,0:T(8,128)(2,1)S(1)}, ...), condition=%wide.region_4.7_spmd.clone, body=%wide.region_3.6_spmd.clone.sunk | while | flops 16877316 | bytes 661863 | solution.py:124
  745.1 4.5 collective-permute-start.14
  749.6 5.3 collective-permute-start.15
  758.3 110.5 %reduce-scatter.11.cloned.1.call-done = f32[8,27,128]{2,0,1:T(8,128)} async-done(((f32[512,27,128]{2,0,1:T(8,128)}), f32[8,27,128]{2,0,1:T(8,128)}) %reduce-scatter.11.cloned.1.call-update) | async-done | bytes 110608 | tf_op jit(solution)/shard_map/reduce_scatter | solution.py:129
  (758 shorter events, 358.1 us)
Async XLA Ops:
  7.2 81.5 %all-gather.5.cloned.1.call-start = ((), (), s32[]{:S(2)}) async-start(), calls=%async_computation.5 | async-start | bytes 3594240 | tf_op jit(solution)/shard_map/all_gather | solution.py:117
  7.9 197.1 %reduce-scatter.5.cloned.1.call-start = ((), (), s32[]{:S(2)}) async-start(), calls=%async_computation.6 | async-start | bytes 983040 | tf_op jit(solution)/shard_map/reduce_scatter | solution.py:79
  88.7 110.1 %copy-start = (s32[3]{0:T(128)S(1)}, s32[3]{0:T(128)}, u32[]{:S(2)}) copy-start(s32[3]{0:T(128)} %constant.387.clone.1) | copy-start | bytes 40
  170.0 102.8 %all-gather.3.cloned.1.call-start = ((), (), s32[]{:S(2)}) async-start(), calls=%async_computation.4 | async-start | bytes 3594240 | tf_op jit(solution)/shard_map/all_gather | solution.py:106
  170.7 515.1 %reduce-scatter.7.cloned.1.call-start = ((), (), s32[]{:S(2)}) async-start(), calls=%async_computation.7 | async-start | bytes 983040 | tf_op jit(solution)/shard_map/reduce_scatter | solution.py:79
  190.8 8.9 %collective-permute-start = (bf16[64,512]{1,0:T(8,128)(2,1)S(1)}, bf16[64,512]{1,0:T(8,128)(2,1)S(1)}, u32[]{:S(2)}, u32[]{:S(2)}) collective-permute-start(bf16[64,512]{1,0:T(8,128)(2,1)S(1)} %get-tuple-element.686), channel_id=1, source_target_pairs={{0,4},{4,8},{8,12},{12,16},{16,20},{20,24},{24,28},{28,32},{32,36}... | collective-permute-start | bytes 196616 | tf_op jit(solution)/shard_map/ppermute | solution.py:14
  192.1 7.6 collective-permute-start.1
  196.2 3.6 collective-permute-start.2
  197.5 7.4 collective-permute-start.3
  205.0 131.3 %slice-start.1 = ((f32[384,128]{1,0:T(8,128)}), f32[128,128]{1,0:T(8,128)S(1)}, s32[]{:S(2)}) async-start(f32[384,128]{1,0:T(8,128)} %reduce-scatter.5.cloned.1.call-done), calls=%async_computation.11 | async-start | bytes 131072 | tf_op jit(solution)/shard_map/slice | solution.py:82
  205.9 130.4 %collective-permute-start.8 = (f32[64,128]{1,0:T(8,128)S(1)}, f32[64,128]{1,0:T(8,128)S(1)}, u32[]{:S(2)}, u32[]{:S(2)}) collective-permute-start(f32[64,128]{1,0:T(8,128)S(1)} %get-tuple-element.678), channel_id=1, source_target_pairs={{4,0},{8,4},{12,8},{16,12},{20,16},{24,20},{28,24},{32,28},{36,32}... | collective-permute-start | bytes 98312 | tf_op jit(solution)/shard_map/ppermute | solution.py:14
  328.5 8.5 collective-permute-start.9
  329.8 7.8 collective-permute-start.10
  332.0 6.4 collective-permute-start.11
  420.4 337.9 %reduce-scatter.9.cloned.1.call-start = ((), (), s32[]{:S(2)}) async-start(), calls=%async_computation.8 | async-start | bytes 7188480 | tf_op jit(solution)/shard_map/reduce_scatter | solution.py:147
  431.7 131.1 %collective-permute-start.4 = (bf16[64,512]{1,0:T(8,128)(2,1)S(1)}, bf16[64,512]{1,0:T(8,128)(2,1)S(1)}, u32[]{:S(2)}, u32[]{:S(2)}) collective-permute-start(bf16[64,512]{1,0:T(8,128)(2,1)S(1)} %get-tuple-element.682), channel_id=1, source_target_pairs={{0,4},{4,8},{8,12},{12,16},{16,20},{20,24},{24,28},{28,32},{32,36}... | collective-permute-start | bytes 196616 | tf_op jit(solution)/shard_map/ppermute | solution.py:14
  433.0 129.8 %collective-permute-start.5 = (bf16[64,512]{1,0:T(8,128)(2,1)S(1)}, bf16[64,512]{1,0:T(8,128)(2,1)S(1)}, u32[]{:S(2)}, u32[]{:S(2)}) collective-permute-start(bf16[64,512]{1,0:T(8,128)(2,1)S(1)} %get-tuple-element.681), channel_id=1, source_target_pairs={{0,8},{4,12},{8,16},{12,20},{16,24},{20,28},{24,32},{28,36},{32,40... | collective-permute-start | bytes 196616 | tf_op jit(solution)/shard_map/ppermute | solution.py:14
  437.3 125.6 %collective-permute-start.6 = (bf16[64,512]{1,0:T(8,128)(2,1)S(1)}, bf16[64,512]{1,0:T(8,128)(2,1)S(1)}, u32[]{:S(2)}, u32[]{:S(2)}) collective-permute-start(bf16[64,512]{1,0:T(8,128)(2,1)S(1)} %get-tuple-element.680), channel_id=1, source_target_pairs={{4,0},{8,4},{12,8},{16,12},{20,16},{24,20},{28,24},{32,28},{36,32}... | collective-permute-start | bytes 196616 | tf_op jit(solution)/shard_map/ppermute | solution.py:14
  438.6 124.3 %collective-permute-start.7 = (bf16[64,512]{1,0:T(8,128)(2,1)S(1)}, bf16[64,512]{1,0:T(8,128)(2,1)S(1)}, u32[]{:S(2)}, u32[]{:S(2)}) collective-permute-start(bf16[64,512]{1,0:T(8,128)(2,1)S(1)} %get-tuple-element.679), channel_id=1, source_target_pairs={{8,0},{12,4},{16,8},{20,12},{24,16},{28,20},{32,24},{36,28},{40,32... | collective-permute-start | bytes 196616 | tf_op jit(solution)/shard_map/ppermute | solution.py:14
  562.8 306.1 %reduce-scatter.11.cloned.1.call-start = ((), (), s32[]{:S(2)}) async-start(), calls=%async_computation.9 | async-start | bytes 7188480 | tf_op jit(solution)/shard_map/reduce_scatter | solution.py:129
  685.8 69.2 %slice-start = ((f32[384,128]{1,0:T(8,128)}), f32[128,128]{1,0:T(8,128)S(1)}, s32[]{:S(2)}) async-start(f32[384,128]{1,0:T(8,128)} %reduce-scatter.7.cloned.1.call-done), calls=%async_computation.10 | async-start | bytes 131072 | tf_op jit(solution)/shard_map/slice | solution.py:82
  686.6 68.3 %collective-permute-start.12 = (f32[64,128]{1,0:T(8,128)S(1)}, f32[64,128]{1,0:T(8,128)S(1)}, u32[]{:S(2)}, u32[]{:S(2)}) collective-permute-start(f32[64,128]{1,0:T(8,128)S(1)} %get-tuple-element.674), channel_id=1, source_target_pairs={{4,0},{8,4},{12,8},{16,12},{20,16},{24,20},{28,24},{32,28},{36,32}... | collective-permute-start | bytes 98312 | tf_op jit(solution)/shard_map/ppermute | solution.py:14
  743.8 11.8 %collective-permute-start.13 = (f32[64,128]{1,0:T(8,128)S(1)}, f32[64,128]{1,0:T(8,128)S(1)}, u32[]{:S(2)}, u32[]{:S(2)}) collective-permute-start(f32[64,128]{1,0:T(8,128)S(1)} %get-tuple-element.673), channel_id=1, source_target_pairs={{8,0},{12,4},{16,8},{20,12},{24,16},{28,20},{32,24},{36,28},{40,32... | collective-permute-start | bytes 98312 | tf_op jit(solution)/shard_map/ppermute | solution.py:14
  745.1 11.2 %collective-permute-start.14 = (f32[64,128]{1,0:T(8,128)S(1)}, f32[64,128]{1,0:T(8,128)S(1)}, u32[]{:S(2)}, u32[]{:S(2)}) collective-permute-start(f32[64,128]{1,0:T(8,128)S(1)} %get-tuple-element.672), channel_id=1, source_target_pairs={{0,4},{4,8},{8,12},{12,16},{16,20},{20,24},{24,28},{28,32},{32,36}... | collective-permute-start | bytes 98312 | tf_op jit(solution)/shard_map/ppermute | solution.py:14
  749.6 7.4 collective-permute-start.15
Sparse Core Ops, SparseCore 0:
  10.6 78.0 all-gather.4
  170.1 23.1 reduce-scatter.4
  195.9 76.8 all-gather.2
  420.5 24.8 reduce-scatter.6
  562.9 154.1 reduce-scatter.8
  721.8 146.9 reduce-scatter.10
where the time goes:
time: 880 us; the launch traced here: 876 us
  waiting for transfers between devices  255 us (29%)
  matrix products  175 us (20%)
  local copies, waits for them, and re-layouts  147 us (17%)
  loops' own time  111 us (13%)
  other arithmetic  106 us (12%)
  starting transfers between devices  37.9 us (4%)
  blocking collectives  22.9 us (3%)
  between operations  22.5 us (3%)
    reduce_scatter x1, waiting for transfers between devices, on_device(): lax.psum_scatter(weight_term(ext_hidden, grad_second), 'space', scatter_d...  111 us
    another operation x2, loops' own time, weight_term(): stacked = lax.map(advance, jnp.arange(27, dtype=jnp.int32))  106 us
    all_gather x1, waiting for transfers between devices, on_device(): second_whole = lax.all_gather(weight_second, 'space', axis=0, tiled=True)  71.8 us
    all_gather x1, waiting for transfers between devices, on_device(): segment = lax.all_gather(weight_first, 'space', axis=0, tiled=True)  65.6 us
    dot_general x54, matrix products, advance(): lax.dot_general(picked, gradient, (((0,), (0,)), ((), ())), preferred_ele...  53.9 us
    scatter-add x27, other arithmetic, backward_step(): return running.at[lookup[offset]].add(contrib)  45.9 us
    scatter-add x27, other arithmetic, advance(): return current.at[lookup[offset]].add(contrib)  45.9 us
    gather x54, local copies, waits for them, and re-layouts, advance(): picked = jnp.take(extended, lookup[offset], axis=0)  45.8 us
  transfers between devices with their start and end apart: 22, of which 5 were waited for; matrix products, arithmetic and copies ran while one was open for 30% of the time, Pallas kernels for 0%

commit v1 on v0

--- a/solution.py
+++ b/solution.py
@@ -61,7 +61,34 @@
         return jnp.take(shaped, lent_table[position], axis=0).reshape(spread * 64, source.shape[1])
 
     def extend(source):
-        gathered = lax.all_gather(source, "chan", axis=1, tiled=True)
+
+        def plan_the_files(x_in):
+            n_now = lax.axis_size("chan")
+            mixed_arr = lax.axis_index("chan")
+            built, f_next, upper = (n_now, mixed_arr, x_in.shape[1])
+            state_next = range(built)
+            tall = map(lambda t: (t, (t + 1) % built), state_next)
+            block_list = list(tall)
+            even = range(built)
+            g_now = map(lambda t: (t, (t - 1) % built), even)
+            sides = list(g_now)
+            after = jnp.zeros((*x_in.shape[:1], built * upper, *x_in.shape[2:]), x_in.dtype)
+            after = lax.dynamic_update_slice_in_dim(after, x_in, f_next * upper, axis=1)
+            side_arr = carry_in = x_in
+            f_now = built // 2
+            for dev_i in range(1, f_now + 1):
+                side_arr = lax.ppermute(side_arr, perm=block_list, axis_name="chan")
+                after = lax.dynamic_update_slice_in_dim(
+                    after, side_arr, (f_next - dev_i) % built * upper, axis=1
+                )
+                if dev_i < built - f_now:
+                    carry_in = lax.ppermute(carry_in, axis_name="chan", perm=sides)
+                    after = lax.dynamic_update_slice_in_dim(
+                        after, carry_in, (f_next + dev_i) % built * upper, axis=1
+                    )
+            return after
+
+        gathered = plan_the_files(source)
         blocks = [gathered]
         for position, offset in enumerate(direction_steps):
             blocks.append(passed_along(outgoing(gathered, position), "space", offset))

time: 880 us -> 783 us (0.89)
  waiting for transfers between devices: 255 us -> 172 us
  blocking collectives: 22.9 us -> 0 us
    reduce_scatter x1, waiting for transfers between devices: 111 us -> 0.01 us  [on_device(): lax.psum_scatter(weight_term(ext_hidden, grad_second), 'space', scatter_d...]
    reduce_scatter x1, waiting for transfers between devices: 0.01 us -> 110 us  [on_device(): lax.psum_scatter(weight_term(ext_in, grad_first), 'space', scatter_dimens...]
    all_gather x1, waiting for transfers between devices: 65.6 us -> 0.02 us  [on_device(): segment = lax.all_gather(weight_first, 'space', axis=0, tiled=True)]
    all_gather x1, waiting for transfers between devices: 71.8 us -> 40.8 us  [on_device(): second_whole = lax.all_gather(weight_second, 'space', axis=0, tiled=True)]
    all_gather x2 -> x0, blocking collectives: 22.9 us -> none  [extend(): gathered = lax.all_gather(source, 'chan', axis=1, tiled=True)]
  transfers between devices with their start and end apart: 22 -> 28, of which waited for: 5 -> 10; matrix products, arithmetic and copies ran while one was open for 30% -> 45% of each run, Pallas kernels for 0% -> 0%
where the time goes in v1:
time: 783 us; the launch traced here: 778 us
  matrix products  175 us (22%)
  waiting for transfers between devices  172 us (22%)
  local copies, waits for them, and re-layouts  148 us (19%)
  loops' own time  111 us (14%)
  other arithmetic  107 us (14%)
  starting transfers between devices  43.3 us (6%)
  between operations  22.5 us (3%)
    reduce_scatter x1, waiting for transfers between devices, on_device(): lax.psum_scatter(weight_term(ext_in, grad_first), 'space', scatter_dimens...  110 us
    another operation x2, loops' own time, weight_term(): stacked = lax.map(advance, jnp.arange(27, dtype=jnp.int32))  106 us
    dot_general x54, matrix products, advance(): lax.dot_general(picked, gradient, (((0,), (0,)), ((), ())), preferred_ele...  54 us
    scatter-add x27, other arithmetic, backward_step(): return running.at[lookup[offset]].add(contrib)  45.9 us
    scatter-add x27, other arithmetic, advance(): return current.at[lookup[offset]].add(contrib)  45.9 us
    gather x54, local copies, waits for them, and re-layouts, advance(): picked = jnp.take(extended, lookup[offset], axis=0)  45.8 us
    all_gather x1, waiting for transfers between devices, on_device(): second_whole = lax.all_gather(weight_second, 'space', axis=0, tiled=True)  40.8 us
    ppermute x16, starting transfers between devices, passed_along(): return lax.ppermute(value, axis, pairs)  35.8 us
  transfers between devices with their start and end apart: 28, of which 10 were waited for; matrix products, arithmetic and copies ran while one was open for 45% of the time, Pallas kernels for 0%

profile of v1, /device:TPU:8, one launch (start us, length us, event | category | flops | bytes accessed | tf_op | source)
XLA Modules:
  0.0 778.2 jit_solution(1520997210466276488)
XLA Ops:
  14.5 3.3 gather_fusion.4
  29.9 3.7 collective-permute-done.2
  35.0 3.1 collective-permute-start.4
  40.7 1.7 collective-permute-done.5
  42.5 5.5 collective-permute-done.6
  48.0 40.8 %all-gather.5.cloned.1.call-done = bf16[512,27,128]{2,0,1:T(8,128)(2,1)} async-done(((bf16[8,27,128]{2,0,1:T(8,128)(2,1)}), bf16[512,27,128]{2,0,1:T(8,128)(2,1)}) %all-gather.5.cloned.1.call-update) | async-done | bytes 3538960 | tf_op jit(solution)/shard_map/all_gather | solution.py:144
  88.9 80.3 %while.83 = (s32[]{:T(128)}, f32[448,512]{1,0:T(8,128)S(1)}, s32[27,128]{1,0:T(8,128)S(1)}, bf16[512,27,128]{2,0,1:T(8,128)(2,1)}, bf16[128,128]{1,0:T(8,128)(2,1)S(1)}, /*index=5*/s32[]{:T(128)}) while((s32[]{:T(128)}, f32[448,512]{1,0:T(8,128)S(1)}, s32[27,128]{1,0:T(8,128)S(1)}, bf16[512,27,128]{2,0,1:T(8,128)(2,1)}, ...), condition=%wide.region_7.10_spmd, body=%wide.region_5.9_spmd.sunk | while | flops 16843136 | bytes 1738325 | solution.py:168
  90.1 1.7 scatter_fusion
  93.1 1.7 scatter_fusion
  96.1 1.7 scatter_fusion
  99.1 1.7 scatter_fusion
  102.0 1.7 scatter_fusion
  105.0 1.7 scatter_fusion
  108.0 1.7 scatter_fusion
  111.0 1.7 scatter_fusion
  113.9 1.7 scatter_fusion
  116.9 1.7 scatter_fusion
  119.9 1.7 scatter_fusion
  122.8 1.7 scatter_fusion
  125.8 1.7 scatter_fusion
  128.8 1.7 scatter_fusion
  131.8 1.7 scatter_fusion
  134.7 1.7 scatter_fusion
  137.7 1.7 scatter_fusion
  140.7 1.7 scatter_fusion
  143.7 1.7 scatter_fusion
  146.7 1.7 scatter_fusion
  149.6 1.7 scatter_fusion
  152.6 1.7 scatter_fusion
  158.6 1.7 scatter_fusion
  161.5 1.7 scatter_fusion
  167.5 1.7 scatter_fusion
  170.3 55.8 %while.87 = (s32[]{:T(128)}, f32[128,128]{1,0:T(8,128)S(1)}, s32[27,128]{1,0:T(8,128)S(1)}, bf16[448,512]{1,0:T(8,128)(2,1)S(1)}, bf16[512,27,128]{2,0,1:T(8,128)(2,1)}, /*index=5*/s32[]{:T(128)}, s32[]{:T(128)}) while((s32[]{:T(128)}, f32[128,128]{1,0:T(8,128)S(1)}, s32[27,128]{1,0:T(8,128)S(1)}, bf16[448,512]{1,0:T(8,128)(2,1)S(1)}, ...), condition=%wide.region_2.5_spmd.clone, body=%wide.region_1.4_spmd.clone.sunk | while | flops 16877316 | bytes 661863 | solution.py:141
  235.4 4.0 collective-permute-start.11
  243.2 5.2 collective-permute-done.13
  251.8 3.0 collective-permute-start.16
  254.8 4.4 collective-permute-start.17
  263.0 80.3 %while.84 = (s32[]{:T(128)}, f32[448,512]{1,0:T(8,128)S(1)}, s32[27,128]{1,0:T(8,128)S(1)}, bf16[512,27,128]{2,0,1:T(8,128)(2,1)}, bf16[128,128]{1,0:T(8,128)(2,1)S(1)}, /*index=5*/s32[]{:T(128)}) while((s32[]{:T(128)}, f32[448,512]{1,0:T(8,128)S(1)}, s32[27,128]{1,0:T(8,128)S(1)}, bf16[512,27,128]{2,0,1:T(8,128)(2,1)}, ...), condition=%wide.region_15.18_spmd, body=%wide.region_13.17_spmd.sunk | while | flops 16843136 | bytes 1738325 | solution.py:188
  267.2 1.7 scatter_fusion.1
  270.2 1.7 scatter_fusion.1
  273.2 1.7 scatter_fusion.1
  276.1 1.7 scatter_fusion.1
  282.1 1.7 scatter_fusion.1
  288.0 1.7 scatter_fusion.1
  291.0 1.7 scatter_fusion.1
  297.0 1.7 scatter_fusion.1
  302.9 1.7 scatter_fusion.1
  305.9 1.7 scatter_fusion.1
  308.8 1.7 scatter_fusion.1
  311.8 1.7 scatter_fusion.1
  317.8 1.7 scatter_fusion.1
  323.7 1.7 scatter_fusion.1
  326.7 1.7 scatter_fusion.1
  329.7 1.7 scatter_fusion.1
  332.6 1.7 scatter_fusion.1
  338.6 1.7 scatter_fusion.1
  344.3 3.7 broadcast.342.clone.1
  348.0 119.1 %while.86 = (s32[]{:T(128)}, f32[27,512,128]{2,1,0:T(8,128)}, s32[27]{0:T(128)S(1)}, s32[27,128]{1,0:T(8,128)S(1)}, bf16[448,512]{1,0:T(8,128)(2,1)S(1)}, /*inde...) while((s32[]{:T(128)}, f32[27,512,128]{2,1,0:T(8,128)}, s32[27]{0:T(128)S(1)}, ...), condition=%wide.region_21.24_spmd, body=%wide.region_20.23_spmd.sunk | while | flops 16844548 | bytes 694683 | solution.py:126
  467.2 3.7 broadcast.342.clone
  470.9 119.2 %while.85 = (s32[]{:T(128)}, f32[27,512,128]{2,1,0:T(8,128)}, s32[27]{0:T(128)S(1)}, s32[27,128]{1,0:T(8,128)S(1)}, bf16[448,512]{1,0:T(8,128)(2,1)S(1)}, /*inde...) while((s32[]{:T(128)}, f32[27,512,128]{2,1,0:T(8,128)}, s32[27]{0:T(128)S(1)}, ...), condition=%wide.region_18.21_spmd, body=%wide.region_17.20_spmd.sunk | while | flops 16844548 | bytes 694683 | solution.py:126
  592.3 55.8 %while.88 = (s32[]{:T(128)}, f32[128,128]{1,0:T(8,128)S(1)}, s32[27,128]{1,0:T(8,128)S(1)}, bf16[448,512]{1,0:T(8,128)(2,1)S(1)}, bf16[512,27,128]{2,0,1:T(8,128)(2,1)}, /*index=5*/s32[]{:T(128)}, s32[]{:T(128)}) while((s32[]{:T(128)}, f32[128,128]{1,0:T(8,128)S(1)}, s32[27,128]{1,0:T(8,128)S(1)}, bf16[448,512]{1,0:T(8,128)(2,1)S(1)}, ...), condition=%wide.region_4.7_spmd.clone, body=%wide.region_3.6_spmd.clone.sunk | while | flops 16877316 | bytes 661863 | solution.py:151
  649.5 3.9 collective-permute-start.20
  653.4 4.4 collective-permute-start.21
  661.2 110.2 %reduce-scatter.9.cloned.1.call-done = f32[8,27,128]{2,0,1:T(8,128)} async-done(((f32[512,27,128]{2,0,1:T(8,128)}), f32[8,27,128]{2,0,1:T(8,128)}) %reduce-scatter.9.cloned.1.call-update) | async-done | bytes 110608 | tf_op jit(solution)/shard_map/reduce_scatter | solution.py:174
  (777 shorter events, 371.5 us)
Async XLA Ops:
  7.2 81.6 %all-gather.5.cloned.1.call-start = ((), (), s32[]{:S(2)}) async-start(), calls=%async_computation.5 | async-start | bytes 3594240 | tf_op jit(solution)/shard_map/all_gather | solution.py:144
  7.9 162.3 %all-gather.3.cloned.1.call-start = ((), (), s32[]{:S(2)}) async-start(), calls=%async_computation.4 | async-start | bytes 3594240 | tf_op jit(solution)/shard_map/all_gather | solution.py:133
  9.5 19.0 %collective-permute-start = (bf16[128,128]{1,0:T(8,128)(2,1)S(1)}, bf16[128,128]{1,0:T(8,128)(2,1)S(1)}, u32[]{:S(2)}, u32[]{:S(2)}) collective-permute-start(bf16[128,128]{1,0:T(8,128)(2,1)S(1)} %get-tuple-element.674), channel_id=1, source_target_pairs={{0,1},{1,2},{2,3},{3,0},{4,5},{5,6},{6,7},{7,4},{8,9},{9,10},{10,1... | collective-permute-start | bytes 98312 | tf_op jit(solution)/shard_map/ppermute | solution.py:80
  11.1 18.8 %collective-permute-start.1 = (bf16[128,128]{1,0:T(8,128)(2,1)S(1)}, bf16[128,128]{1,0:T(8,128)(2,1)S(1)}, u32[]{:S(2)}, u32[]{:S(2)}) collective-permute-start(bf16[128,128]{1,0:T(8,128)(2,1)S(1)} %get-tuple-element.674), channel_id=1, source_target_pairs={{0,3},{1,0},{2,1},{3,2},{4,7},{5,4},{6,5},{7,6},{8,11},{9,8},{10,9... | collective-permute-start | bytes 98312 | tf_op jit(solution)/shard_map/ppermute | solution.py:85
  11.9 236.5 %reduce-scatter.5.cloned.1.call-start = ((), (), s32[]{:S(2)}) async-start(), calls=%async_computation.6 | async-start | bytes 983040 | tf_op jit(solution)/shard_map/reduce_scatter | solution.py:106
  28.5 5.1 collective-permute-start.2
  33.7 7.0 collective-permute-start.3
  35.0 5.7 collective-permute-start.4
  38.1 4.4 collective-permute-start.5
  39.4 8.6 %collective-permute-start.6 = (bf16[64,512]{1,0:T(8,128)(2,1)S(1)}, bf16[64,512]{1,0:T(8,128)(2,1)S(1)}, u32[]{:S(2)}, u32[]{:S(2)}) collective-permute-start(bf16[64,512]{1,0:T(8,128)(2,1)S(1)} %get-tuple-element.687), channel_id=1, source_target_pairs={{8,0},{12,4},{16,8},{20,12},{24,16},{28,20},{32,24},{36,28},{40,32... | collective-permute-start | bytes 196616 | tf_op jit(solution)/shard_map/ppermute | solution.py:14
  169.2 58.5 %copy-start = (s32[3]{0:T(128)S(1)}, s32[3]{0:T(128)}, u32[]{:S(2)}) copy-start(s32[3]{0:T(128)} %constant.425.clone.1) | copy-start | bytes 40
  170.2 420.0 %reduce-scatter.7.cloned.1.call-start = ((), (), s32[]{:S(2)}) async-start(), calls=%async_computation.7 | async-start | bytes 983040 | tf_op jit(solution)/shard_map/reduce_scatter | solution.py:106
  226.2 4.0 collective-permute-start.7
  228.6 3.9 collective-permute-start.8
  230.2 3.9 collective-permute-start.9
  234.1 7.9 %collective-permute-start.10 = (bf16[64,512]{1,0:T(8,128)(2,1)S(1)}, bf16[64,512]{1,0:T(8,128)(2,1)S(1)}, u32[]{:S(2)}, u32[]{:S(2)}) collective-permute-start(bf16[64,512]{1,0:T(8,128)(2,1)S(1)} %get-tuple-element.686), channel_id=1, source_target_pairs={{0,4},{4,8},{8,12},{12,16},{16,20},{20,24},{24,28},{28,32},{32,36}... | collective-permute-start | bytes 196616 | tf_op jit(solution)/shard_map/ppermute | solution.py:14
  235.4 6.6 collective-permute-start.11
  239.4 3.7 collective-permute-start.12
  240.7 7.6 collective-permute-start.13
  249.2 10.9 %collective-permute-start.14 = (f32[64,128]{1,0:T(8,128)S(1)}, f32[64,128]{1,0:T(8,128)S(1)}, u32[]{:S(2)}, u32[]{:S(2)}) collective-permute-start(f32[64,128]{1,0:T(8,128)S(1)} %get-tuple-element.682), channel_id=1, source_target_pairs={{4,0},{8,4},{12,8},{16,12},{20,16},{24,20},{28,24},{32,28},{36,32}... | collective-permute-start | bytes 98312 | tf_op jit(solution)/shard_map/ppermute | solution.py:14
  250.5 10.3 %collective-permute-start.15 = (f32[64,128]{1,0:T(8,128)S(1)}, f32[64,128]{1,0:T(8,128)S(1)}, u32[]{:S(2)}, u32[]{:S(2)}) collective-permute-start(f32[64,128]{1,0:T(8,128)S(1)} %get-tuple-element.681), channel_id=1, source_target_pairs={{8,0},{12,4},{16,8},{20,12},{24,16},{28,20},{32,24},{36,28},{40,32... | collective-permute-start | bytes 98312 | tf_op jit(solution)/shard_map/ppermute | solution.py:14
  251.8 9.6 %collective-permute-start.16 = (f32[64,128]{1,0:T(8,128)S(1)}, f32[64,128]{1,0:T(8,128)S(1)}, u32[]{:S(2)}, u32[]{:S(2)}) collective-permute-start(f32[64,128]{1,0:T(8,128)S(1)} %get-tuple-element.680), channel_id=1, source_target_pairs={{0,4},{4,8},{8,12},{12,16},{16,20},{20,24},{24,28},{28,32},{32,36}... | collective-permute-start | bytes 98312 | tf_op jit(solution)/shard_map/ppermute | solution.py:14
  254.8 7.3 collective-permute-start.17
  344.2 317.0 %reduce-scatter.11.cloned.1.call-start = ((), (), s32[]{:S(2)}) async-start(), calls=%async_computation.9 | async-start | bytes 7188480 | tf_op jit(solution)/shard_map/reduce_scatter | solution.py:156
  467.2 304.2 %reduce-scatter.9.cloned.1.call-start = ((), (), s32[]{:S(2)}) async-start(), calls=%async_computation.8 | async-start | bytes 7188480 | tf_op jit(solution)/shard_map/reduce_scatter | solution.py:174
  590.2 67.6 %slice-start = ((f32[384,128]{1,0:T(8,128)}), f32[128,128]{1,0:T(8,128)S(1)}, s32[]{:S(2)}) async-start(f32[384,128]{1,0:T(8,128)} %reduce-scatter.7.cloned.1.call-done), calls=%async_computation.10 | async-start | bytes 131072 | tf_op jit(solution)/shard_map/slice | solution.py:109
  591.0 66.8 %collective-permute-start.18 = (f32[64,128]{1,0:T(8,128)S(1)}, f32[64,128]{1,0:T(8,128)S(1)}, u32[]{:S(2)}, u32[]{:S(2)}) collective-permute-start(f32[64,128]{1,0:T(8,128)S(1)} %get-tuple-element.678), channel_id=1, source_target_pairs={{4,0},{8,4},{12,8},{16,12},{20,16},{24,20},{28,24},{32,28},{36,32}... | collective-permute-start | bytes 98312 | tf_op jit(solution)/shard_map/ppermute | solution.py:14
  648.2 10.3 %collective-permute-start.19 = (f32[64,128]{1,0:T(8,128)S(1)}, f32[64,128]{1,0:T(8,128)S(1)}, u32[]{:S(2)}, u32[]{:S(2)}) collective-permute-start(f32[64,128]{1,0:T(8,128)S(1)} %get-tuple-element.677), channel_id=1, source_target_pairs={{8,0},{12,4},{16,8},{20,12},{24,16},{28,20},{32,24},{36,28},{40,32... | collective-permute-start | bytes 98312 | tf_op jit(solution)/shard_map/ppermute | solution.py:14
  649.5 9.6 %collective-permute-start.20 = (f32[64,128]{1,0:T(8,128)S(1)}, f32[64,128]{1,0:T(8,128)S(1)}, u32[]{:S(2)}, u32[]{:S(2)}) collective-permute-start(f32[64,128]{1,0:T(8,128)S(1)} %get-tuple-element.676), channel_id=1, source_target_pairs={{0,4},{4,8},{8,12},{12,16},{16,20},{20,24},{24,28},{28,32},{32,36}... | collective-permute-start | bytes 98312 | tf_op jit(solution)/shard_map/ppermute | solution.py:14
  653.4 6.5 collective-permute-start.21
Sparse Core Ops, SparseCore 0:
  10.6 78.1 all-gather.4
  91.3 74.3 all-gather.2
  170.3 21.9 reduce-scatter.4
  344.4 26.3 reduce-scatter.6
  467.3 152.3 reduce-scatter.10
  624.4 146.9 reduce-scatter.8
